TPU v7x, 128 devices: a whole 4x4x4 slice. The times are simulated.
128 devices in a mesh: row: 4 (over z_hi, core), col: 32 (over x, z_lo, y).
Axes of the slice: x: 4, y: 4, z: 4 (z_hi: 2, z_lo: 2; z = z_hi * 2 + z_lo), core: 2. Of those that a mesh axis runs over, the one named last changes fastest.
Arguments:
- right_side: float32 [131072, 128], P(('row', 'col')), may hold values from -150 to 150
- block_values: bfloat16 [64, 917504], P(None, ('row', 'col')), may hold values from -1 to 2, as said below
- block_cols: int32 [14336], P(('row', 'col')), may hold values from 0 to 511, as said below
- row_ptrs: int32 [8320], P(('row', 'col')), may hold values from 0 to 112, as said below
- precond: float32 [131072, 1024], P(('row', 'col')), may hold values from -1 to 2, as said below
Outputs:
- solution: float32 [131072, 128], P(('row', 'col'))
- residual: float32 [131072, 128], P(('row', 'col'))
Inputs may be any that keep to these rules, and one draw needn't show every extreme that they name: `row_ptrs`: in each tile t the 65 pointers from index t * (65) on never fall, start at 0 and end at 112. `block_cols`: each of the 2048 block rows of A holds 7 blocks. `block_values`: with the pattern, the blocks form a symmetric matrix A. `precond`: each 1024 x 1024 block is lower triangular with a positive diagonal.
All inputs are finite; a program needn't handle non-finite values.
Results may differ from a plain program's by a relative error of at most 0.0076.
Values may be sent and summed in bfloat16 or wider, within the bound.
A program may use at most 128 MiB of HBM per device.

v0:
```python
import jax
import jax.numpy as jnp
from jax import lax
from jax.sharding import PartitionSpec as P

ITERS = 2


def per_device(right_side, block_values, block_cols, row_ptrs, precond):
    block_size = block_values.shape[0]
    slot_count = block_cols.shape[0]
    tile_rows = row_ptrs.shape[0] - 1
    seg_rows = right_side.shape[0]
    rhs_count = right_side.shape[1]
    tile_cols = lax.axis_size("col") * (seg_rows // block_size)
    tile_blocks = block_values.reshape(block_size, slot_count, block_size)
    slot_index = jnp.arange(slot_count, dtype=jnp.int32)
    slot_rows = jnp.sum((slot_index[:, None] >= row_ptrs[None, 1:]).astype(jnp.int32), axis=1)
    solution = jnp.zeros_like(right_side)
    residual = right_side
    direction = right_side
    image_vec = right_side
    alpha_prev = jnp.ones((rhs_count,), jnp.float32)
    gamma_prev = jnp.ones((rhs_count,), jnp.float32)
    for iteration in range(ITERS):
        half_step = jnp.dot(
            precond, residual, precision=lax.Precision.HIGHEST, preferred_element_type=jnp.float32
        )
        smoothed = lax.dot_general(
            precond,
            half_step,
            (((0,), (0,)), ((), ())),
            precision=lax.Precision.HIGHEST,
            preferred_element_type=jnp.float32,
        )
        local_energy = jnp.sum(residual * smoothed, axis=0)
        gamma_now = lax.psum(local_energy, ("row", "col"))
        gathered = lax.all_gather(smoothed.astype(jnp.bfloat16), "col", axis=0, tiled=True)
        pieces = gathered.reshape(tile_cols, block_size, rhs_count)[block_cols]
        products = jnp.einsum(
            "ibj,bjk->bik", tile_blocks, pieces, preferred_element_type=jnp.float32
        )
        partial_value = jax.ops.segment_sum(
            products, slot_rows, num_segments=tile_rows, indices_are_sorted=True
        )
        applied = lax.psum_scatter(
            partial_value.reshape(tile_rows * block_size, rhs_count),
            "row",
            scatter_dimension=0,
            tiled=True,
        )
        delta_now = lax.psum(jnp.sum(smoothed * applied, axis=0), ("row", "col"))
        if iteration == 0:
            alpha_now = gamma_now / delta_now
            direction = smoothed
            image_vec = applied
        else:
            beta_now = gamma_now / gamma_prev
            alpha_now = gamma_now / (delta_now - beta_now * gamma_now / alpha_prev)
            direction = smoothed + beta_now * direction
            image_vec = applied + beta_now * image_vec
        solution = solution + alpha_now * direction
        residual = residual - alpha_now * image_vec
        gamma_prev = gamma_now
        alpha_prev = alpha_now
    return (solution, residual)


def solution(mesh):
    return jax.shard_map(
        per_device,
        mesh=mesh,
        in_specs=(
            P(("row", "col"), None),
            P(None, ("row", "col")),
            P(("row", "col")),
            P(("row", "col")),
            P(("row", "col"), None),
        ),
        out_specs=(P(("row", "col"), None), P(("row", "col"), None)),
        check_vma=False,
    )
```

profile of v0, /device:TPU:1, one launch (start us, length us, event | category | flops | bytes accessed | tf_op | source)
XLA Modules:
  0.0 653.4 jit_solution(4864520073481413777)
XLA Ops:
  7.2 5.4 fusion.5
  12.7 3.2 fusion.3
  16.0 2.3 reshape.24
  18.5 148.9 %all-gather.3.cloned.1.call-done = bf16[32768,128]{0,1:T(8,128)(2,1)} async-done(((bf16[1024,128]{0,1:T(8,128)(2,1)}), bf16[32768,128]{0,1:T(8,128)(2,1)}) %all-gather.3.cloned.1.call-update) | async-done | bytes 8388624 | tf_op jit(solution)/shard_map/all_gather | solution.py:38
  167.4 11.9 %copy.26 = bf16[32768,128]{1,0:T(8,128)(2,1)} copy(bf16[32768,128]{0,1:T(8,128)(2,1)} %all-gather.3.cloned.1.call-done) | data formatting | bytes 16777216 | tf_op jit(solution)/shard_map/all_gather | solution.py:38
  179.3 5.4 gather_fusion
  184.7 3.9 convolution_bitcast_fusion.1
  188.9 11.9 %scatter_fusion = f32[64,64,128]{2,1,0:T(8,128)S(1)} fusion(f32[64,64,128]{2,1,0:T(8,128)S(1)} %broadcast.13.clone, s32[112]{0:T(128)S(1)} %convert_reduce_fusion, f32[112,64,128]{2,1,0:T(8,128)} %convolution_bitcast_fusion.1), kind=kCustom, calls=%fused_computation.2 | custom fusion | flops 917504 | bytes 11010496 | tf_op jit(solution)/shard_map/scatter-add | solution.py:43
  200.8 1.9 copy.28
  203.9 57.5 %reduce-scatter.3.cloned.1.call-done = f32[1024,128]{0,1:T(8,128)} async-done(((f32[4096,128]{0,1:T(8,128)}), f32[1024,128]{0,1:T(8,128)}) %reduce-scatter.3.cloned.1.call-update) | async-done | bytes 524304 | tf_op jit(solution)/shard_map/reduce_scatter | solution.py:46
  261.4 1.2 multiply_reduce_fusion.2
  262.6 64.9 %all-reduce.1 = (f32[128]{0:T(128)S(1)}, f32[128]{0:T(128)S(1)}) all-reduce(f32[128]{0:T(128)S(1)} %get-tuple-element.11, f32[128]{0:T(128)S(1)} %get-tuple-element.10), channel_id=1, replica_groups=mesh['row'=4,'col'=32] {'row','col'}, use_global_device_ids=true, to_apply=%region_1.0 | all-reduce | flops 256 | bytes 2048 | tf_op jit(solution)/shard_map/psum | solution.py:37
  327.5 6.9 %fusion.2 = f32[128,1024]{1,0:T(8,128)S(1)} fusion(f32[1024,1024]{1,0:T(8,128)} %param.9, f32[1024,128]{0,1:T(8,128)S(1)} %copy.25, f32[1024,128]{0,1:T(8,128)} %reduce-scatter.3.cloned.1.call-done, f32[128]{0:T(128)S(1)} %div.12), kind=kOutput, calls=%fused_computation.22 | convolution fusion | flops 1610874880 | bytes 5767680 | tf_op jit(solution)/shard_map/dot_general | solution.py:26
  334.5 3.3 fusion.4
  337.8 145.3 %all-gather.5.cloned.1.call-done = bf16[32768,128]{0,1:T(8,128)(2,1)} async-done(((bf16[1024,128]{0,1:T(8,128)(2,1)}), bf16[32768,128]{0,1:T(8,128)(2,1)}) %all-gather.5.cloned.1.call-update) | async-done | bytes 8388624 | tf_op jit(solution)/shard_map/all_gather | solution.py:38
  483.2 11.9 %copy.30 = bf16[32768,128]{1,0:T(8,128)(2,1)} copy(bf16[32768,128]{0,1:T(8,128)(2,1)} %all-gather.5.cloned.1.call-done) | data formatting | bytes 16777216 | tf_op jit(solution)/shard_map/all_gather | solution.py:38
  495.1 5.6 gather_fusion.1
  500.7 3.9 convolution_bitcast_fusion
  504.9 11.9 %scatter_fusion.1 = f32[64,64,128]{2,1,0:T(8,128)S(1)} fusion(f32[64,64,128]{2,1,0:T(8,128)S(1)} %broadcast.13, s32[112]{0:T(128)S(1)} %convert_reduce_fusion, f32[112,64,128]{2,1,0:T(8,128)} %convolution_bitcast_fusion), kind=kCustom, calls=%fused_computation.3 | custom fusion | flops 917504 | bytes 11010496 | tf_op jit(solution)/shard_map/scatter-add | solution.py:43
  516.8 1.9 copy.32
  518.7 58.8 %reduce-scatter.5.cloned.1.call-done = f32[1024,128]{0,1:T(8,128)} async-done(((f32[4096,128]{0,1:T(8,128)}), f32[1024,128]{0,1:T(8,128)}) %reduce-scatter.5.cloned.1.call-update) | async-done | bytes 524304 | tf_op jit(solution)/shard_map/reduce_scatter | solution.py:46
  577.5 1.3 multiply_reduce_fusion
  578.7 64.7 %all-reduce = (f32[128]{0:T(128)S(1)}, f32[128]{0:T(128)S(1)}) all-reduce(f32[128]{0:T(128)S(1)} %get-tuple-element.9, f32[128]{0:T(128)S(1)} %get-tuple-element.8), channel_id=1, replica_groups=mesh['row'=4,'col'=32] {'row','col'}, use_global_device_ids=true, to_apply=%region_8.0 | all-reduce | flops 256 | bytes 2048 | tf_op jit(solution)/shard_map/psum | solution.py:37
  643.5 1.4 multiply_subtract_fusion
  (37 shorter events, 4.1 us)
Async XLA Ops:
  7.2 160.2 %all-gather.3.cloned.1.call-start = ((), (), s32[]{:S(2)}) async-start(), calls=%async_computation.2 | async-start | bytes 8650752 | tf_op jit(solution)/shard_map/all_gather | solution.py:38
  7.2 5.5 copy-start
  12.7 3.3 copy-start.7
  15.9 2.4 copy-start.8
  15.9 245.5 %reduce-scatter.3.cloned.1.call-start = ((), (), s32[]{:S(2)}) async-start(), calls=%async_computation.3 | async-start | bytes 2621440 | tf_op jit(solution)/shard_map/reduce_scatter | solution.py:46
  18.3 166.4 %copy-start.2 = (bf16[64,112,64]{2,1,0:T(8,128)(2,1)}, bf16[64,112,64]{2,1,0:T(8,128)(2,1)S(1)}, u32[]{:S(2)}) copy-start(bf16[64,112,64]{2,1,0:T(8,128)(2,1)S(1)} %reshape.24) | copy-start | bytes 2752516
  202.6 1.0 copy-start.6
  202.7 280.5 %all-gather.5.cloned.1.call-start = ((), (), s32[]{:S(2)}) async-start(), calls=%async_computation.4 | async-start | bytes 8650752 | tf_op jit(solution)/shard_map/all_gather | solution.py:38
  327.5 6.9 %copy-start.1 = (f32[1024,1024]{1,0:T(8,128)S(1)}, f32[1024,1024]{1,0:T(8,128)}, u32[]{:S(2)}) copy-start(f32[1024,1024]{1,0:T(8,128)} %param.9) | copy-start | bytes 12582916
  337.8 239.7 %reduce-scatter.5.cloned.1.call-start = ((), (), s32[]{:S(2)}) async-start(), calls=%async_computation.5 | async-start | bytes 2621440 | tf_op jit(solution)/shard_map/reduce_scatter | solution.py:46
  495.1 5.6 copy-start.3
  518.7 58.8 %copy-start.4 = (f32[1024,128]{0,1:T(8,128)S(1)}, f32[1024,128]{0,1:T(8,128)}, u32[]{:S(2)}) copy-start(f32[1024,128]{0,1:T(8,128)} %reduce-scatter.3.cloned.1.call-done) | copy-start | bytes 1572868
  518.7 58.8 %copy-start.5 = (f32[1024,128]{0,1:T(8,128)S(1)}, f32[1024,128]{0,1:T(8,128)}, u32[]{:S(2)}) copy-start(f32[1024,128]{0,1:T(8,128)} %get-tuple-element.23) | copy-start | bytes 1572868
Sparse Core Ops, SparseCore 0:
  16.0 151.3 all-gather.2
  202.8 58.5 reduce-scatter.2
  337.9 145.2 all-gather.4
  518.8 58.6 reduce-scatter.4
where the time goes:
time: 655 us; the launch traced here: 653 us
  waiting for transfers between devices  411 us (63%)
  blocking collectives  130 us (20%)
  local copies, waits for them, and re-layouts  44.6 us (7%)
  other arithmetic  27.8 us (4%)
  matrix products  26.7 us (4%)
  between operations  13.9 us (2%)
    all_gather x2, waiting for transfers between devices, per_device(): lax.all_gather(smoothed.astype(jnp.bfloat16), 'col', axis=0, tiled=True)  294 us
    psum x2, blocking collectives, per_device(): gamma_now = lax.psum(local_energy, ('row', 'col'))  130 us
    reduce_scatter x2, waiting for transfers between devices, per_device(): lax.psum_scatter(partial_value.reshape(tile_rows * block_size, rhs_count)...  116 us
    scatter-add x2, other arithmetic, per_device(): jax.ops.segment_sum(products, slot_rows, num_segments=tile_rows, indices_...  23.8 us
    all_gather x2, local copies, waits for them, and re-layouts, per_device(): lax.all_gather(smoothed.astype(jnp.bfloat16), 'col', axis=0, tiled=True)  23.8 us
  transfers between devices with their start and end apart: 4, of which 4 were waited for; matrix products, arithmetic and copies ran while one was open for 0% of the time, Pallas kernels for 0%

commit v1 on v0

--- a/solution.py
+++ b/solution.py
@@ -34,7 +34,9 @@
             preferred_element_type=jnp.float32,
         )
         local_energy = jnp.sum(residual * smoothed, axis=0)
-        gamma_now = lax.psum(local_energy, ("row", "col"))
+        gamma_now = local_energy
+        for name in ("col", "row"):
+            gamma_now = lax.psum(gamma_now, name)
         gathered = lax.all_gather(smoothed.astype(jnp.bfloat16), "col", axis=0, tiled=True)
         pieces = gathered.reshape(tile_cols, block_size, rhs_count)[block_cols]
         products = jnp.einsum(

time: 655 us -> 827 us (1.26)
  blocking collectives: 130 us -> 304 us
    psum x2 -> x6, blocking collectives: 130 us -> 304 us  [the longest x4 175 us: per_device(): gamma_now = lax.psum(gamma_now, name)]
where the time goes in v1:
time: 827 us; the launch traced here: 825 us
  waiting for transfers between devices  408 us (49%)
  blocking collectives  304 us (37%)
  local copies, waits for them, and re-layouts  44.6 us (5%)
  other arithmetic  27.8 us (3%)
  matrix products  26.6 us (3%)
  between operations  13.9 us (2%)
    all_gather x2, waiting for transfers between devices, per_device(): lax.all_gather(smoothed.astype(jnp.bfloat16), 'col', axis=0, tiled=True)  292 us
    psum x4, blocking collectives, per_device(): gamma_now = lax.psum(gamma_now, name)  175 us
    psum x2, blocking collectives, per_device(): delta_now = lax.psum(jnp.sum(smoothed * applied, axis=0), ('row', 'col'))  130 us
    reduce_scatter x2, waiting for transfers between devices, per_device(): lax.psum_scatter(partial_value.reshape(tile_rows * block_size, rhs_count)...  116 us
    scatter-add x2, other arithmetic, per_device(): jax.ops.segment_sum(products, slot_rows, num_segments=tile_rows, indices_...  23.8 us
    all_gather x2, local copies, waits for them, and re-layouts, per_device(): lax.all_gather(smoothed.astype(jnp.bfloat16), 'col', axis=0, tiled=True)  23.8 us
  transfers between devices with their start and end apart: 4, of which 4 were waited for; matrix products, arithmetic and copies ran while one was open for 0% of the time, Pallas kernels for 0%

profile of v1, /device:TPU:1, one launch (start us, length us, event | category | flops | bytes accessed | tf_op | source)
XLA Modules:
  0.0 825.3 jit_solution(1791332664712663598)
XLA Ops:
  7.2 5.4 fusion.5
  12.7 3.1 fusion.3
  16.0 2.3 reshape.24
  18.4 148.9 %all-gather.3.cloned.1.call-done = bf16[32768,128]{0,1:T(8,128)(2,1)} async-done(((bf16[1024,128]{0,1:T(8,128)(2,1)}), bf16[32768,128]{0,1:T(8,128)(2,1)}) %all-gather.3.cloned.1.call-update) | async-done | bytes 8388624 | tf_op jit(solution)/shard_map/all_gather | solution.py:40
  167.3 11.9 %copy.26 = bf16[32768,128]{1,0:T(8,128)(2,1)} copy(bf16[32768,128]{0,1:T(8,128)(2,1)} %all-gather.3.cloned.1.call-done) | data formatting | bytes 16777216 | tf_op jit(solution)/shard_map/all_gather | solution.py:40
  179.2 5.4 gather_fusion
  184.7 3.9 convolution_bitcast_fusion.1
  188.8 11.9 %scatter_fusion = f32[64,64,128]{2,1,0:T(8,128)S(1)} fusion(f32[64,64,128]{2,1,0:T(8,128)S(1)} %broadcast.13.clone, s32[112]{0:T(128)S(1)} %convert_reduce_fusion, f32[112,64,128]{2,1,0:T(8,128)} %convolution_bitcast_fusion.1), kind=kCustom, calls=%fused_computation.2 | custom fusion | flops 917504 | bytes 11010496 | tf_op jit(solution)/shard_map/scatter-add | solution.py:45
  200.8 1.9 copy.28
  203.9 57.5 %reduce-scatter.3.cloned.1.call-done = f32[1024,128]{0,1:T(8,128)} async-done(((f32[4096,128]{0,1:T(8,128)}), f32[1024,128]{0,1:T(8,128)}) %reduce-scatter.3.cloned.1.call-update) | async-done | bytes 524304 | tf_op jit(solution)/shard_map/reduce_scatter | solution.py:48
  262.6 64.8 %psum.44 = f32[128]{0:T(128)S(1)} all-reduce(f32[128]{0:T(128)S(1)} %get-tuple-element.10), channel_id=1, replica_groups=mesh['row'=4,'col'=32] {'row','col'}, use_global_device_ids=true, to_apply=%region_7.0 | all-reduce | flops 128 | bytes 1024 | tf_op jit(solution)/shard_map/psum | solution.py:54
  327.4 66.0 %psum.42 = f32[128]{0:T(128)S(1)} all-reduce(f32[128]{0:T(128)S(1)} %get-tuple-element.11), channel_id=1, replica_groups=mesh['row'=4,'col'=32] {'col'}, use_global_device_ids=true, to_apply=%region_1.0 | all-reduce | flops 128 | bytes 1024 | tf_op jit(solution)/shard_map/psum | solution.py:39
  393.4 21.3 %psum.43 = f32[128]{0:T(128)S(1)} all-reduce(f32[128]{0:T(128)S(1)} %psum.42), channel_id=1, replica_groups=mesh['row'=4,'col'=32] {'row'}, use_global_device_ids=true, to_apply=%region_2.0 | all-reduce | flops 128 | bytes 1024 | tf_op jit(solution)/shard_map/psum | solution.py:39
  414.7 6.9 fusion.2
  421.7 3.3 fusion.4
  425.0 142.7 %all-gather.5.cloned.1.call-done = bf16[32768,128]{0,1:T(8,128)(2,1)} async-done(((bf16[1024,128]{0,1:T(8,128)(2,1)}), bf16[32768,128]{0,1:T(8,128)(2,1)}) %all-gather.5.cloned.1.call-update) | async-done | bytes 8388624 | tf_op jit(solution)/shard_map/all_gather | solution.py:40
  567.8 11.9 %copy.30 = bf16[32768,128]{1,0:T(8,128)(2,1)} copy(bf16[32768,128]{0,1:T(8,128)(2,1)} %all-gather.5.cloned.1.call-done) | data formatting | bytes 16777216 | tf_op jit(solution)/shard_map/all_gather | solution.py:40
  579.7 5.6 gather_fusion.1
  585.3 3.9 convolution_bitcast_fusion
  589.5 11.9 %scatter_fusion.1 = f32[64,64,128]{2,1,0:T(8,128)S(1)} fusion(f32[64,64,128]{2,1,0:T(8,128)S(1)} %broadcast.13, s32[112]{0:T(128)S(1)} %convert_reduce_fusion, f32[112,64,128]{2,1,0:T(8,128)} %convolution_bitcast_fusion), kind=kCustom, calls=%fused_computation.3 | custom fusion | flops 917504 | bytes 11010496 | tf_op jit(solution)/shard_map/scatter-add | solution.py:45
  603.3 58.8 %reduce-scatter.5.cloned.1.call-done = f32[1024,128]{0,1:T(8,128)} async-done(((f32[4096,128]{0,1:T(8,128)}), f32[1024,128]{0,1:T(8,128)}) %reduce-scatter.5.cloned.1.call-update) | async-done | bytes 524304 | tf_op jit(solution)/shard_map/reduce_scatter | solution.py:48
  663.3 64.7 %psum.47 = f32[128]{0:T(128)S(1)} all-reduce(f32[128]{0:T(128)S(1)} %get-tuple-element.8), channel_id=1, replica_groups=mesh['row'=4,'col'=32] {'row','col'}, use_global_device_ids=true, to_apply=%region_14.0 | all-reduce | flops 128 | bytes 1024 | tf_op jit(solution)/shard_map/psum | solution.py:54
  728.1 66.0 %psum.45 = f32[128]{0:T(128)S(1)} all-reduce(f32[128]{0:T(128)S(1)} %get-tuple-element.9), channel_id=1, replica_groups=mesh['row'=4,'col'=32] {'col'}, use_global_device_ids=true, to_apply=%region_9.0 | all-reduce | flops 128 | bytes 1024 | tf_op jit(solution)/shard_map/psum | solution.py:39
  794.1 21.2 %psum.46 = f32[128]{0:T(128)S(1)} all-reduce(f32[128]{0:T(128)S(1)} %psum.45), channel_id=1, replica_groups=mesh['row'=4,'col'=32] {'row'}, use_global_device_ids=true, to_apply=%region_10.0 | all-reduce | flops 128 | bytes 1024 | tf_op jit(solution)/shard_map/psum | solution.py:39
  (41 shorter events, 9.8 us)
Async XLA Ops:
  7.2 160.2 %all-gather.3.cloned.1.call-start = ((), (), s32[]{:S(2)}) async-start(), calls=%async_computation.2 | async-start | bytes 8650752 | tf_op jit(solution)/shard_map/all_gather | solution.py:40
  7.2 5.5 copy-start
  12.7 3.2 copy-start.7
  15.8 2.4 copy-start.8
  15.9 245.5 %reduce-scatter.3.cloned.1.call-start = ((), (), s32[]{:S(2)}) async-start(), calls=%async_computation.3 | async-start | bytes 2621440 | tf_op jit(solution)/shard_map/reduce_scatter | solution.py:48
  18.3 166.4 %copy-start.2 = (bf16[64,112,64]{2,1,0:T(8,128)(2,1)}, bf16[64,112,64]{2,1,0:T(8,128)(2,1)S(1)}, u32[]{:S(2)}) copy-start(bf16[64,112,64]{2,1,0:T(8,128)(2,1)S(1)} %reshape.24) | copy-start | bytes 2752516
  202.6 1.0 copy-start.6
  202.6 365.1 %all-gather.5.cloned.1.call-start = ((), (), s32[]{:S(2)}) async-start(), calls=%async_computation.4 | async-start | bytes 8650752 | tf_op jit(solution)/shard_map/all_gather | solution.py:40
  414.7 6.9 copy-start.1
  425.0 237.1 %reduce-scatter.5.cloned.1.call-start = ((), (), s32[]{:S(2)}) async-start(), calls=%async_computation.5 | async-start | bytes 2621440 | tf_op jit(solution)/shard_map/reduce_scatter | solution.py:48
  579.7 5.6 copy-start.3
  603.3 58.8 %copy-start.4 = (f32[1024,128]{0,1:T(8,128)S(1)}, f32[1024,128]{0,1:T(8,128)}, u32[]{:S(2)}) copy-start(f32[1024,128]{0,1:T(8,128)} %reduce-scatter.3.cloned.1.call-done) | copy-start | bytes 1572868
  603.3 58.8 %copy-start.5 = (f32[1024,128]{0,1:T(8,128)S(1)}, f32[1024,128]{0,1:T(8,128)}, u32[]{:S(2)}) copy-start(f32[1024,128]{0,1:T(8,128)} %get-tuple-element.19) | copy-start | bytes 1572868
Sparse Core Ops, SparseCore 0:
  16.0 151.3 all-gather.2
  202.8 58.5 reduce-scatter.2
  425.1 142.6 all-gather.4
  603.4 58.6 reduce-scatter.4
